TPU v7x, 32 devices: a whole 2x2x4 slice. The times are simulated.
32 devices in a mesh: rows: 8 (over y, x, core), depth: 4 (over z).
Axes of the slice: x: 2, y: 2, z: 4, core: 2. Of those that a mesh axis runs over, the one named last changes fastest.
Arguments:
- left_factors: bfloat16 [8, 8, 2048, 128], P('rows', 'depth'), may hold values from -0.125 to 0.125
- right_factors: bfloat16 [8, 8, 2048, 128], P('rows', 'depth'), may hold values from -0.125 to 0.125
- probe_matrix: bfloat16 [2048, 128], replicated, may hold values from -6 to 6
- tile_list: int32 [8, 4], replicated, may hold values from 0 to 7, all different within a row
Outputs:
- basis: float32 [8, 4, 2048, 128], P('rows', None, 'depth')
- chol_factor: float32 [8, 4, 128, 128], P('rows')
Inputs may be any that keep to these rules, and one draw needn't show every extreme that they name: `tile_list`: each row holds 4 different tile rows, and every tile row is named by some row.
All inputs are finite; a program needn't handle non-finite values.
Results may differ from a plain program's by a relative error of at most 0.0058.
Values may be sent and summed in bfloat16 or wider, within the bound.
No kernel may reach another device: no remote copies, remote signals or barrier semaphores. Data moves between devices by JAX's collectives and lax.ppermute only.
A program may use at most 64 MiB of HBM per device.

v0:
```python
import math
import jax
import jax.numpy as jnp
from jax import lax
from jax.sharding import PartitionSpec as P


def on_device(left_factors, right_factors, probe_matrix, tile_list):
    left_own = left_factors[0]
    right_own = right_factors[0]
    panels, tile_size, rank_size = left_own.shape
    scale = math.sqrt(float(tile_size))
    image = jnp.einsum(
        "pbk,bl->pkl", left_own, probe_matrix, preferred_element_type=jnp.float32
    ).astype(jnp.bfloat16)
    sketch_rows = jnp.einsum(
        "pbk,pkl->pbl", right_own, image, preferred_element_type=jnp.float32
    ).astype(jnp.bfloat16)
    sliced = lax.all_to_all(sketch_rows[:, None], "rows", split_axis=2, concat_axis=1, tiled=True)
    readers_order = jnp.transpose(tile_list)
    outgoing = jnp.take(sliced, readers_order, axis=1)
    arrived = lax.all_to_all(outgoing, "rows", split_axis=2, concat_axis=2, tiled=True)
    listed = arrived.shape[1]
    arrived = arrived.reshape(panels, listed, tile_size, rank_size)
    coupling = jnp.einsum(
        "pbk,ptbl->tpkl", right_own, arrived, preferred_element_type=jnp.float32
    ).astype(jnp.bfloat16)
    partial_sketch = jnp.einsum(
        "pbk,tpkl->tbl", left_own, coupling, preferred_element_type=jnp.float32
    )
    own_rows = lax.psum_scatter(partial_sketch, "depth", scatter_dimension=1, tiled=True)
    gram_part = jnp.einsum("tbk,tbl->tkl", own_rows, own_rows, precision=lax.Precision.HIGHEST)
    gram = lax.psum(gram_part, "depth")
    lower = jnp.linalg.cholesky(gram)
    solved = jax.scipy.linalg.solve_triangular(
        lower, jnp.transpose(own_rows, (0, 2, 1)), lower=True
    )
    basis = jnp.transpose(solved, (0, 2, 1)) * scale
    return (basis[None], (lower / scale)[None])


def solution(mesh):
    in_specs = (P("rows", "depth", None, None), P("rows", "depth", None, None), P(), P())
    out_specs = (P("rows", None, "depth", None), P("rows", None, None, None))
    return jax.shard_map(
        on_device, mesh=mesh, in_specs=in_specs, out_specs=out_specs, check_vma=False
    )
```

profile of v0, /device:TPU:0, one launch (start us, length us, event | category | flops | bytes accessed | tf_op | source)
XLA Modules:
  0.0 313.9 jit_solution(2542688194420749601)
XLA Ops:
  7.2 0.0 copy-start
  7.2 1.2 copy-done
  8.4 0.0 copy-start.3
  8.4 2.3 fusion.3
  10.7 2.0 copy.43
  12.7 5.2 %all-to-all-start = ((bf16[2,1,2048,128]{3,0,1,2:T(2,128)(2,1)}), bf16[2,1,2048,128]{3,0,1,2:T(2,128)(2,1)S(1)}, u32[]{:S(2)}, u32[]{:S(2)}) async-start(bf16[2,1,2048,128]{3,0,1,2:T(2,128)(2,1)} %copy.43), calls=%async_computation | async-start | bytes 2097152 | tf_op jit(solution)/shard_map/all_to_all | solution.py:19
  17.9 0.0 reduce-scatter.2.cloned.1.call-start
  17.9 0.0 copy-done.3
  18.0 0.1 reshape.29
  18.0 0.1 copy.40
  18.2 15.1 %all-to-all-done = bf16[2,1,2048,128]{3,0,1,2:T(2,128)(2,1)S(1)} async-done(((bf16[2,1,2048,128]{3,0,1,2:T(2,128)(2,1)}), bf16[2,1,2048,128]{3,0,1,2:T(2,128)(2,1)S(1)}, u32[]{:S(2)}, u32[]{:S(2)}) %all-to-all-start) | async-done | bytes 1048608 | tf_op jit(solution)/shard_map/all_to_all | solution.py:19
  33.3 0.1 copy.44
  33.4 3.0 gather_fusion
  36.4 2.6 fusion.2
  39.1 51.5 %all_to_all.17 = bf16[2,4,8,256,128]{4,3,1,0,2:T(8,128)(2,1)S(1)} all-to-all(bf16[2,4,8,256,128]{4,3,1,0,2:T(8,128)(2,1)S(1)} %fusion.2), channel_id=1, replica_groups=mesh['rows'=8,'depth'=4] {'rows'}, dimensions={2} | all-to-all | bytes 8388608 | tf_op jit(solution)/shard_map/all_to_all | solution.py:22
  90.6 2.2 copy.46
  92.8 0.0 copy-done.2
  92.9 6.1 %convolution_bitcast_fusion = f32[4,2048,128]{1,2,0:T(8,128)} fusion(bf16[1,2,2048,128]{3,2,1,0:T(8,128)(2,1)S(1)} %copy-done, bf16[2,4,2048,128]{3,2,1,0:T(8,128)(2,1)} %bitcast.59, bf16[1,2,2048,128]{3,2,1,0:T(8,128)(2,1)S(1)} %copy-done.2), kind=kOutput, calls=%fused_computation.5 | convolution fusion | flops 1073872896 | bytes 10485760 | tf_op jit(solution)/shard_map/pbk,tpkl->tbl/dot_general | solution.py:28
  99.0 0.0 reduce-scatter.2.cloned.1.call-update
  99.0 0.2 all-reduce.2.cloned.1.call-start
  99.2 76.1 %reduce-scatter.2.cloned.1.call-done = f32[4,512,128]{1,2,0:T(8,128)} async-done(((f32[4,2048,128]{1,2,0:T(8,128)}), f32[4,512,128]{1,2,0:T(8,128)}) %reduce-scatter.2.cloned.1.call-update) | async-done | bytes 1048592 | tf_op jit(solution)/shard_map/reduce_scatter | solution.py:31
  175.3 3.5 %fusion.24 = f32[4,128,128]{1,2,0:T(8,128)} fusion(f32[4,512,128]{1,2,0:T(8,128)} %reduce-scatter.2.cloned.1.call-done), kind=kOutput, calls=%fused_computation.31 | convolution fusion | flops 402653184 | bytes 1310720 | tf_op jit(solution)/shard_map/tbk,tbl->tkl/dot_general | solution.py:32
  178.8 0.0 all-reduce.2.cloned.1.call-update
  178.9 36.2 %all-reduce.2.cloned.1.call-done = f32[4,128,128]{1,2,0:T(8,128)} async-done(((f32[4,128,128]{1,2,0:T(8,128)}), f32[4,128,128]{1,2,0:T(8,128)}) %all-reduce.2.cloned.1.call-update) | async-done | bytes 262160 | tf_op jit(solution)/shard_map/psum | solution.py:33
  215.1 1.1 copy.50
  216.1 1.0 fusion.23
  217.1 46.9 %custom-call.8 = f32[4,128,128]{2,1,0:T(8,128)S(1)} custom-call(f32[4,128,128]{2,1,0:T(8,128)S(1)} %fusion.23), custom_call_target="Cholesky" | custom-call | tf_op jit(solution)/shard_map/jit(cholesky)/cholesky | solution.py:34
  264.1 0.1 compare_reduce_fusion
  264.2 0.8 multiply_bitcast_fusion
  265.0 39.3 %custom-call.9 = f32[4,1,128,128]{2,3,1,0:T(8,128)S(1)} custom-call(f32[4,1,128,128]{3,2,1,0:T(8,128)S(1)} %get-tuple-element.3), custom_call_target="InvertDiagBlocksLowerTriangular" | custom-call | tf_op jit(solution)/shard_map/jit(_solve_triangular)/vmap()/triangular_solve | solution.py:35
  304.3 0.0 copy-done.1
  304.3 2.8 fusion.4
  (8 shorter events, 0.1 us)
Async XLA Ops:
  7.2 1.2 copy-start
  8.4 9.5 %copy-start.3 = (s32[8,4]{0,1:T(4,128)S(1)}, s32[8,4]{0,1:T(4,128)}, u32[]{:S(2)}) copy-start(s32[8,4]{0,1:T(4,128)} %param.7) | copy-start | bytes 388
  12.7 20.6 %all-to-all-start = ((bf16[2,1,2048,128]{3,0,1,2:T(2,128)(2,1)}), bf16[2,1,2048,128]{3,0,1,2:T(2,128)(2,1)S(1)}, u32[]{:S(2)}, u32[]{:S(2)}) async-start(bf16[2,1,2048,128]{3,0,1,2:T(2,128)(2,1)} %copy.43), calls=%async_computation | async-start | bytes 2097152 | tf_op jit(solution)/shard_map/all_to_all | solution.py:19
  17.9 157.4 %reduce-scatter.2.cloned.1.call-start = ((), (), s32[]{:S(2)}) async-start(), calls=%async_computation.3 | async-start | bytes 5242880 | tf_op jit(solution)/shard_map/reduce_scatter | solution.py:31
  90.6 2.2 copy-start.2
  99.0 116.0 %all-reduce.2.cloned.1.call-start = ((), (), s32[]{:S(2)}) async-start(), calls=%async_computation.4 | async-start | bytes 524288 | tf_op jit(solution)/shard_map/psum | solution.py:33
  175.3 129.0 %copy-start.1 = (f32[4,512,128]{1,2,0:T(8,128)S(1)}, f32[4,512,128]{1,2,0:T(8,128)}, u32[]{:S(2)}) copy-start(f32[4,512,128]{1,2,0:T(8,128)} %reduce-scatter.2.cloned.1.call-done) | copy-start | bytes 3145732
Sparse Core Ops, SparseCore 0:
  99.1 76.1 reduce-scatter.1
  178.9 36.0 all-reduce.1
where the time goes:
time: 314 us
  waiting for transfers between devices  127 us (40%)
  other arithmetic  90.9 us (29%)
  blocking collectives  51.5 us (16%)
  matrix products  14.7 us (5%)
  between operations  14.1 us (4%)
  local copies, waits for them, and re-layouts  9.88 us (3%)
  starting transfers between devices  5.46 us (2%)
    reduce_scatter x1, waiting for transfers between devices, on_device(): lax.psum_scatter(partial_sketch, 'depth', scatter_dimension=1, tiled=True)  76.1 us
    all_to_all x1, blocking collectives, on_device(): lax.all_to_all(outgoing, 'rows', split_axis=2, concat_axis=2, tiled=True)  51.5 us
    another operation x4, other arithmetic, on_device(): lower = jnp.linalg.cholesky(gram)  47.1 us
    another operation x2, other arithmetic, on_device(): jax.scipy.linalg.solve_triangular(lower, jnp.transpose(own_rows, (0, 2, 1...  39.3 us
    psum x1, waiting for transfers between devices, on_device(): gram = lax.psum(gram_part, 'depth')  36.2 us
    all_to_all x1, waiting for transfers between devices, on_device(): lax.all_to_all(sketch_rows[:, None], 'rows', split_axis=2, concat_axis=1,...  15.1 us
  transfers between devices with their start and end apart: 3, of which 3 were waited for; matrix products, arithmetic and copies ran while one was open for 0% of the time, Pallas kernels for 0%

commit v1 on v0

--- a/solution.py
+++ b/solution.py
@@ -30,7 +30,8 @@
     )
     own_rows = lax.psum_scatter(partial_sketch, "depth", scatter_dimension=1, tiled=True)
     gram_part = jnp.einsum("tbk,tbl->tkl", own_rows, own_rows, precision=lax.Precision.HIGHEST)
-    gram = lax.psum(gram_part, "depth")
+    terms = lax.all_gather(gram_part, "depth")
+    gram = jnp.sum(terms, axis=0)
     lower = jnp.linalg.cholesky(gram)
     solved = jax.scipy.linalg.solve_triangular(
         lower, jnp.transpose(own_rows, (0, 2, 1)), lower=True

time: 314 us -> 306 us (0.975)
  waiting for transfers between devices: 127 us -> 120 us
    psum x1 -> x0, waiting for transfers between devices: 36.2 us -> none  [on_device(): gram = lax.psum(gram_part, 'depth')]
    all_gather x0 -> x1, waiting for transfers between devices: none -> 28.6 us  [on_device(): terms = lax.all_gather(gram_part, 'depth')]
where the time goes in v1:
time: 306 us
  waiting for transfers between devices  120 us (39%)
  other arithmetic  91.2 us (30%)
  blocking collectives  51.5 us (17%)
  matrix products  14.6 us (5%)
  between operations  14.1 us (5%)
  local copies, waits for them, and re-layouts  8.93 us (3%)
  starting transfers between devices  5.46 us (2%)
    reduce_scatter x1, waiting for transfers between devices, on_device(): lax.psum_scatter(partial_sketch, 'depth', scatter_dimension=1, tiled=True)  76.1 us
    all_to_all x1, blocking collectives, on_device(): lax.all_to_all(outgoing, 'rows', split_axis=2, concat_axis=2, tiled=True)  51.5 us
    another operation x4, other arithmetic, on_device(): lower = jnp.linalg.cholesky(gram)  47.1 us
    another operation x2, other arithmetic, on_device(): jax.scipy.linalg.solve_triangular(lower, jnp.transpose(own_rows, (0, 2, 1...  39.3 us
    all_gather x1, waiting for transfers between devices, on_device(): terms = lax.all_gather(gram_part, 'depth')  28.6 us
    all_to_all x1, waiting for transfers between devices, on_device(): lax.all_to_all(sketch_rows[:, None], 'rows', split_axis=2, concat_axis=1,...  15.1 us
    dot_general x1, matrix products, on_device(): jnp.einsum('pbk,tpkl->tbl', left_own, coupling, preferred_element_type=jn...  6.14 us
  transfers between devices with their start and end apart: 3, of which 3 were waited for; matrix products, arithmetic and copies ran while one was open for 0% of the time, Pallas kernels for 0%

profile of v1, /device:TPU:0, one launch (start us, length us, event | category | flops | bytes accessed | tf_op | source)
XLA Modules:
  0.0 305.7 jit_solution(12468124127899089897)
XLA Ops:
  7.2 0.0 copy-start
  7.2 1.2 copy-done
  8.4 0.0 copy-start.3
  8.4 2.3 fusion.3
  10.7 2.0 copy.39
  12.7 5.2 %all-to-all-start = ((bf16[2,1,2048,128]{3,0,1,2:T(2,128)(2,1)}), bf16[2,1,2048,128]{3,0,1,2:T(2,128)(2,1)S(1)}, u32[]{:S(2)}, u32[]{:S(2)}) async-start(bf16[2,1,2048,128]{3,0,1,2:T(2,128)(2,1)} %copy.39), calls=%async_computation | async-start | bytes 2097152 | tf_op jit(solution)/shard_map/all_to_all | solution.py:19
  17.9 0.0 reduce-scatter.2.cloned.1.call-start
  17.9 0.0 copy-done.3
  18.0 0.1 reshape.29
  18.0 0.1 copy.36
  18.2 15.1 %all-to-all-done = bf16[2,1,2048,128]{3,0,1,2:T(2,128)(2,1)S(1)} async-done(((bf16[2,1,2048,128]{3,0,1,2:T(2,128)(2,1)}), bf16[2,1,2048,128]{3,0,1,2:T(2,128)(2,1)S(1)}, u32[]{:S(2)}, u32[]{:S(2)}) %all-to-all-start) | async-done | bytes 1048608 | tf_op jit(solution)/shard_map/all_to_all | solution.py:19
  33.3 0.1 copy.40
  33.4 3.0 gather_fusion
  36.4 2.6 fusion.2
  39.1 51.5 %all_to_all.17 = bf16[2,4,8,256,128]{4,3,1,0,2:T(8,128)(2,1)S(1)} all-to-all(bf16[2,4,8,256,128]{4,3,1,0,2:T(8,128)(2,1)S(1)} %fusion.2), channel_id=1, replica_groups=mesh['rows'=8,'depth'=4] {'rows'}, dimensions={2} | all-to-all | bytes 8388608 | tf_op jit(solution)/shard_map/all_to_all | solution.py:22
  90.6 2.2 copy.42
  92.8 0.0 copy-done.2
  92.9 6.1 %convolution_bitcast_fusion = f32[4,2048,128]{1,2,0:T(8,128)} fusion(bf16[1,2,2048,128]{3,2,1,0:T(8,128)(2,1)S(1)} %copy-done, bf16[2,4,2048,128]{3,2,1,0:T(8,128)(2,1)} %bitcast.60, bf16[1,2,2048,128]{3,2,1,0:T(8,128)(2,1)S(1)} %copy-done.2), kind=kOutput, calls=%fused_computation.5 | convolution fusion | flops 1073872896 | bytes 10485760 | tf_op jit(solution)/shard_map/pbk,tpkl->tbl/dot_general | solution.py:28
  99.0 0.0 reduce-scatter.2.cloned.1.call-update
  99.0 0.2 all-gather.3.cloned.1.call-start
  99.2 76.1 %reduce-scatter.2.cloned.1.call-done = f32[4,512,128]{1,2,0:T(8,128)} async-done(((f32[4,2048,128]{1,2,0:T(8,128)}), f32[4,512,128]{1,2,0:T(8,128)}) %reduce-scatter.2.cloned.1.call-update) | async-done | bytes 1048592 | tf_op jit(solution)/shard_map/reduce_scatter | solution.py:31
  175.3 3.4 %fusion.24 = f32[4,128,128]{2,1,0:T(8,128)} fusion(f32[4,512,128]{1,2,0:T(8,128)} %reduce-scatter.2.cloned.1.call-done), kind=kOutput, calls=%fused_computation.31 | convolution fusion | flops 402653184 | bytes 1310720 | tf_op jit(solution)/shard_map/tbk,tbl->tkl/dot_general | solution.py:32
  178.8 0.0 all-gather.3.cloned.1.call-update
  178.8 28.6 %all-gather.3.cloned.1.call-done = f32[16,128,128]{2,1,0:T(8,128)} async-done(((f32[4,128,128]{2,1,0:T(8,128)}), f32[16,128,128]{2,1,0:T(8,128)}) %all-gather.3.cloned.1.call-update) | async-done | bytes 1048592 | tf_op jit(solution)/shard_map/all_gather | solution.py:33
  207.4 1.3 reduce_sum.9
  208.7 0.1 copy.45
  208.9 46.9 %custom-call.8 = f32[4,128,128]{2,1,0:T(8,128)S(1)} custom-call(f32[4,128,128]{2,1,0:T(8,128)S(1)} %fusion.23), custom_call_target="Cholesky" | custom-call | tf_op jit(solution)/shard_map/jit(cholesky)/cholesky | solution.py:35
  255.9 0.1 compare_reduce_fusion
  256.0 0.8 multiply_bitcast_fusion
  256.8 39.3 %custom-call.9 = f32[4,1,128,128]{2,3,1,0:T(8,128)S(1)} custom-call(f32[4,1,128,128]{3,2,1,0:T(8,128)S(1)} %get-tuple-element.3), custom_call_target="InvertDiagBlocksLowerTriangular" | custom-call | tf_op jit(solution)/shard_map/jit(_solve_triangular)/vmap()/triangular_solve | solution.py:36
  296.1 0.0 copy-done.1
  296.1 2.8 fusion.4
  (9 shorter events, 0.1 us)
Async XLA Ops:
  7.2 1.2 copy-start
  8.4 9.5 %copy-start.3 = (s32[8,4]{0,1:T(4,128)S(1)}, s32[8,4]{0,1:T(4,128)}, u32[]{:S(2)}) copy-start(s32[8,4]{0,1:T(4,128)} %param.7) | copy-start | bytes 388
  12.7 20.6 %all-to-all-start = ((bf16[2,1,2048,128]{3,0,1,2:T(2,128)(2,1)}), bf16[2,1,2048,128]{3,0,1,2:T(2,128)(2,1)S(1)}, u32[]{:S(2)}, u32[]{:S(2)}) async-start(bf16[2,1,2048,128]{3,0,1,2:T(2,128)(2,1)} %copy.39), calls=%async_computation | async-start | bytes 2097152 | tf_op jit(solution)/shard_map/all_to_all | solution.py:19
  17.9 157.4 %reduce-scatter.2.cloned.1.call-start = ((), (), s32[]{:S(2)}) async-start(), calls=%async_computation.3 | async-start | bytes 5242880 | tf_op jit(solution)/shard_map/reduce_scatter | solution.py:31
  90.6 2.2 copy-start.2
  99.0 108.4 %all-gather.3.cloned.1.call-start = ((), (), s32[]{:S(2)}) async-start(), calls=%async_computation.4 | async-start | bytes 1310720 | tf_op jit(solution)/shard_map/all_gather | solution.py:33
  175.3 120.8 %copy-start.1 = (f32[4,512,128]{1,2,0:T(8,128)S(1)}, f32[4,512,128]{1,2,0:T(8,128)}, u32[]{:S(2)}) copy-start(f32[4,512,128]{1,2,0:T(8,128)} %reduce-scatter.2.cloned.1.call-done) | copy-start | bytes 3145732
Sparse Core Ops, SparseCore 0:
  99.1 76.1 reduce-scatter.1
  178.9 28.4 all-gather.2
